TPU v7x, 512 devices: a whole 4x8x8 slice. The times are simulated.
512 devices in a mesh: seq: 64 (over z_hi, x, y), width: 8 (over z_lo, core).
Axes of the slice: x: 4, y: 8, z: 8 (z_hi: 2, z_lo: 4; z = z_hi * 4 + z_lo), core: 2. Of those that a mesh axis runs over, the one named last changes fastest.
Arguments:
- projected: bfloat16 [32768, 3, 4096], P('seq', None, 'width'), may hold values from -6 to 6
- short_filter: float32 [3, 3, 4096], P(None, None, 'width'), may hold values from -3.5 to 3.5
- long_filter: bfloat16 [256, 128], P('width'), may hold values from -0.5 to 0.5
- out_weight: bfloat16 [4096, 4096], P('seq', 'width'), may hold values from -0.09375 to 0.09375
Outputs:
- mixed: bfloat16 [32768, 4096], P('seq', 'width')
All inputs are finite; a program needn't handle non-finite values.
Results may differ from a plain program's by a relative error of at most 0.0057.
Values may be sent and summed in bfloat16 or wider, within the bound.
No kernel may reach another device: no remote copies, remote signals or barrier semaphores. Data moves between devices by JAX's collectives and lax.ppermute only.
A program may use at most 64 MiB of HBM per device.

v0:
```python
import jax
import jax.numpy as jnp
from jax import lax
from jax.sharding import PartitionSpec as P


def from_behind(array, axis, by):
    devices = lax.axis_size(axis)
    pairs = [(i, i + by) for i in range(devices) if 0 <= i + by < devices]
    return lax.ppermute(array, axis, pairs)


def featurize_joined(joined, short_filter):
    values = joined.astype(jnp.float32)
    return (
        short_filter[0] * values[2:]
        + short_filter[1] * values[1:-1]
        + short_filter[2] * values[:-2]
    )


def toeplitz_of(long_filter):
    span = long_filter.shape[1]
    row_ids = jnp.arange(span, dtype=jnp.int32)[:, None]
    col_ids = jnp.arange(2 * span - 1, dtype=jnp.int32)[None, :]
    tap_index = row_ids - col_ids + (span - 1)
    inside = (tap_index >= 0) & (tap_index < span)
    picked = jnp.take(long_filter, jnp.clip(tap_index, 0, span - 1), axis=1)
    return jnp.where(inside[None], picked, jnp.zeros_like(picked))


def long_conv(extended, toeplitz, out_rows):
    span = toeplitz.shape[1]
    groups = toeplitz.shape[0]
    channels = extended.shape[1]

    def one_block(block_index):
        window_rows = lax.dynamic_slice_in_dim(extended, block_index * span, 2 * span - 1, 0)
        window_rows = window_rows.reshape(2 * span - 1, groups, channels // groups)
        result = jnp.einsum(
            "gij,jgc->igc", toeplitz, window_rows, preferred_element_type=jnp.float32
        )
        return result.reshape(span, channels)

    blocks = lax.map(one_block, jnp.arange(out_rows // span, dtype=jnp.int32))
    return blocks.reshape(out_rows, channels)


def on_device(projected, short_filter, long_filter, out_weight):
    tok_rows = projected.shape[0]
    span = long_filter.shape[1]
    tail_rows = projected[tok_rows - span - 1 :]
    previous = from_behind(tail_rows, "seq", 1)
    joined = jnp.concatenate([previous, projected], axis=0)
    featured = featurize_joined(joined, short_filter)
    extended = (featured[:, 1] * featured[:, 2]).astype(jnp.bfloat16)
    query = featured[span - 1 :, 0]
    filtered = long_conv(extended, toeplitz_of(long_filter), tok_rows)
    gated = (query * filtered).astype(jnp.bfloat16)
    gathered = lax.all_gather(gated, "width", axis=1, tiled=True)
    mixed = jnp.dot(
        gathered,
        lax.all_gather(out_weight, "seq", axis=0, tiled=True),
        preferred_element_type=jnp.float32,
    )
    return mixed.astype(jnp.bfloat16)


def solution(mesh):
    in_specs = (
        P("seq", None, "width"),
        P(None, None, "width"),
        P("width", None),
        P("seq", "width"),
    )
    out_specs = P("seq", "width")
    return jax.shard_map(
        on_device, mesh=mesh, in_specs=in_specs, out_specs=out_specs, check_vma=False
    )
```

profile of v0, /device:TPU:2, one launch (start us, length us, event | category | flops | bytes accessed | tf_op | source)
XLA Modules:
  0.0 351.0 jit_solution(13737784177788745816)
XLA Ops:
  6.5 0.0 all-gather.3.cloned.1.call-start
  6.5 1.1 slice.31
  7.6 3.5 collective-permute-start
  11.2 0.7 slice_bitcast_fusion.3
  11.9 0.3 reshape.76
  12.3 0.8 copy.9
  13.1 65.9 %gather_fusion = bf16[32640,32]{1,0:T(8,128)(2,1)} fusion(bf16[32,128]{0,1:T(8,128)(2,1)S(1)} %copy.9, s32[32768]{0:T(1024)S(1)} %pad_clamp_fusion), kind=kCustom, calls=%fused_computation | custom fusion | bytes 4308480 | tf_op jit(solution)/shard_map/jit(_take)/gather | solution.py:28
  79.0 6.9 %copy.10 = bf16[32640,32]{0,1:T(8,128)(2,1)S(1)} copy(bf16[32640,32]{1,0:T(8,128)(2,1)} %gather_fusion) | data formatting | bytes 4177920 | tf_op jit(solution)/shard_map/jit(_take)/gather | solution.py:28
  85.8 7.8 %reshape.79 = bf16[128,255,32]{1,0,2:T(8,128)(2,1)} reshape(bf16[32640,32]{0,1:T(8,128)(2,1)S(1)} %copy.10) | data formatting | bytes 4177920 | tf_op jit(solution)/shard_map/jit(_take)/gather | solution.py:28
  93.6 0.0 copy-start.1
  93.6 0.1 fusion.10
  93.7 1.9 select_bitcast_fusion
  95.7 0.0 collective-permute-done
  95.7 0.0 copy-done.1
  95.7 0.6 maximum_convert_fusion
  96.3 1.2 fusion
  97.4 0.0 copy-start
  97.4 1.9 copy-done
  99.3 0.2 fusion.5
  99.5 12.1 %while.10 = (s32[]{:T(128)}, f32[4,128,512]{2,1,0:T(8,128)}, s32[4]{0:T(128)S(1)}, bf16[639,512]{1,0:T(8,128)(2,1)S(1)}, bf16[32,128,255]{2,1,0:T(8,128)(2,1)S(1...) while((s32[]{:T(128)}, f32[4,128,512]{2,1,0:T(8,128)}, s32[4]{0:T(128)S(1)}, ...), condition=%wide.region_1.2_spmd, body=%wide.region_0.1_spmd.sunk | while | flops 33423364 | bytes 4705947 | solution.py:45
  99.5 0.6 dynamic_slice.11
  100.8 0.1 constant_dynamic-slice_fusion.2
  100.9 0.1 copy.18
  101.0 0.6 fusion.22
  101.6 0.2 copy.19
  101.8 0.8 constant_dynamic-update-slice_fusion.2
  102.6 0.6 dynamic_slice.11
  103.8 0.1 constant_dynamic-slice_fusion.2
  103.9 0.1 copy.18
  104.0 0.6 fusion.22
  104.7 0.2 copy.19
  104.8 0.7 constant_dynamic-update-slice_fusion.2
  105.6 0.6 dynamic_slice.11
  106.9 0.1 constant_dynamic-slice_fusion.2
  106.9 0.1 copy.18
  107.1 0.6 fusion.22
  107.7 0.2 copy.19
  107.9 0.7 constant_dynamic-update-slice_fusion.2
  108.6 0.6 dynamic_slice.11
  109.9 0.1 constant_dynamic-slice_fusion.2
  110.0 0.1 copy.18
  110.1 0.6 fusion.22
  110.7 0.2 copy.19
  110.9 0.7 constant_dynamic-update-slice_fusion.2
  111.6 2.6 fusion.4
  114.2 0.0 all-gather.3.cloned.1.call-update
  114.2 0.0 all-gather.5.cloned.1.call-start
  114.3 0.7 all-gather.5.cloned.1.call-update
  115.0 60.9 %all-gather.3.cloned.1.call-done = bf16[512,4096]{1,0:T(8,128)(2,1)} async-done(((bf16[512,512]{1,0:T(8,128)(2,1)}), bf16[512,4096]{1,0:T(8,128)(2,1)}) %all-gather.3.cloned.1.call-update) | async-done | bytes 4194320 | tf_op jit(solution)/shard_map/all_gather | solution.py:60
  175.9 161.7 %all-gather.5.cloned.1.call-done = bf16[4096,512]{1,0:T(8,128)(2,1)} async-done(((bf16[64,512]{1,0:T(8,128)(2,1)}), bf16[4096,512]{1,0:T(8,128)(2,1)}) %all-gather.5.cloned.1.call-update) | async-done | bytes 4194320 | tf_op jit(solution)/shard_map/all_gather | solution.py:63
  337.6 6.6 %convolution_convert_fusion = bf16[512,512]{1,0:T(8,128)(2,1)} fusion(bf16[512,4096]{1,0:T(8,128)(2,1)} %all-gather.3.cloned.1.call-done, bf16[4096,512]{1,0:T(8,128)(2,1)} %all-gather.5.cloned.1.call-done), kind=kOutput, calls=%fused_computation.12 | convolution fusion | flops 2147745792 | bytes 8912896 | tf_op jit(solution)/shard_map/dot_general | solution.py:61
  (4 shorter events, 0.1 us)
Async XLA Ops:
  6.5 169.4 %all-gather.3.cloned.1.call-start = ((), (), s32[]{:S(2)}) async-start(), calls=%async_computation | async-start | bytes 4718592 | tf_op jit(solution)/shard_map/all_gather | solution.py:60
  7.6 88.0 %collective-permute-start = (bf16[129,3,512]{2,0,1:T(8,128)(2,1)S(1)}, bf16[129,3,512]{2,0,1:T(8,128)(2,1)S(1)}, u32[]{:S(2)}, u32[]{:S(2)}) collective-permute-start(bf16[129,3,512]{2,0,1:T(8,128)(2,1)S(1)} %slice.31), channel_id=1, source_target_pairs={{0,8},{8,16},{16,24},{24,32},{32,40},{40,48},{48,56},{56,64},{64,7... | collective-permute-start | bytes 1188872 | tf_op jit(solution)/shard_map/ppermute | solution.py:10
  93.6 2.0 copy-start.1
  97.4 1.9 copy-start
  114.2 223.3 %all-gather.5.cloned.1.call-start = ((), (), s32[]{:S(2)}) async-start(), calls=%async_computation.1 | async-start | bytes 4259840 | tf_op jit(solution)/shard_map/all_gather | solution.py:63
Sparse Core Ops, SparseCore 0:
  114.4 61.5 all-gather.2
  180.4 157.0 all-gather.4
where the time goes:
time: 351 us
  waiting for transfers between devices  223 us (64%)
  local copies, waits for them, and re-layouts  92.3 us (26%)
  between operations  13.5 us (4%)
  matrix products  9.11 us (3%)
  other arithmetic  6.61 us (2%)
  starting transfers between devices  3.53 us (1%)
    all_gather x1, waiting for transfers between devices, on_device(): lax.all_gather(out_weight, 'seq', axis=0, tiled=True)  162 us
    gather x3, local copies, waits for them, and re-layouts, toeplitz_of(): picked = jnp.take(long_filter, jnp.clip(tap_index, 0, span - 1), axis=1)  80.5 us
    all_gather x1, waiting for transfers between devices, on_device(): gathered = lax.all_gather(gated, 'width', axis=1, tiled=True)  60.9 us
  transfers between devices with their start and end apart: 3, of which 2 were waited for; matrix products, arithmetic and copies ran while one was open for 24% of the time, Pallas kernels for 0%

commit v1 on v0

--- a/solution.py
+++ b/solution.py
@@ -57,7 +57,9 @@
     query = featured[span - 1 :, 0]
     filtered = long_conv(extended, toeplitz_of(long_filter), tok_rows)
     gated = (query * filtered).astype(jnp.bfloat16)
-    gathered = lax.all_gather(gated, "width", axis=1, tiled=True)
+    gathered = jnp.concatenate(
+        lax.all_to_all(jnp.stack([gated] * lax.axis_size("width")), "width", 0, 0), axis=1
+    )
     mixed = jnp.dot(
         gathered,
         lax.all_gather(out_weight, "seq", axis=0, tiled=True),

time: 351 us -> 254 us (0.72)
  the two profiles are of different devices: /device:TPU:2 before, /device:TPU:1 now
where the time goes in v1:
time: 254 us
  blocking collectives  126 us (50%)
  local copies, waits for them, and re-layouts  93.2 us (37%)
  between operations  13.5 us (5%)
  matrix products  9.16 us (4%)
  other arithmetic  5.83 us (2%)
  starting transfers between devices  4.06 us (2%)
  loops' own time  2.68 us (1%)
    all_to_all x1, blocking collectives, on_device(): lax.all_to_all(jnp.stack([gated] * lax.axis_size('width')), 'width', 0, 0)  126 us
    gather x3, local copies, waits for them, and re-layouts, toeplitz_of(): picked = jnp.take(long_filter, jnp.clip(tap_index, 0, span - 1), axis=1)  80.9 us
    dot_general x1, matrix products, on_device(): jnp.dot(gathered, lax.all_gather(out_weight, 'seq', axis=0, tiled=True),...  6.61 us
  transfers between devices with their start and end apart: 2, of which 0 were waited for; matrix products, arithmetic and copies ran while one was open for 39% of the time, Pallas kernels for 0%

profile of v1, /device:TPU:1, one launch (start us, length us, event | category | flops | bytes accessed | tf_op | source)
XLA Modules:
  0.0 254.0 jit_solution(12429368098740300533)
XLA Ops:
  6.5 0.0 all-gather.2.cloned.1.call-start
  6.5 1.1 slice.31
  7.6 4.1 %collective-permute-start = (bf16[129,3,512]{2,0,1:T(8,128)(2,1)S(1)}, bf16[129,3,512]{2,0,1:T(8,128)(2,1)S(1)}, u32[]{:S(2)}, u32[]{:S(2)}) collective-permute-start(bf16[129,3,512]{2,0,1:T(8,128)(2,1)S(1)} %slice.31), channel_id=1, source_target_pairs={{0,8},{8,16},{16,24},{24,32},{32,40},{40,48},{48,56},{56,64},{64,7... | collective-permute-start | bytes 1188872 | tf_op jit(solution)/shard_map/ppermute | solution.py:10
  11.7 0.0 all-gather.2.cloned.1.call-update
  11.8 0.7 slice_bitcast_fusion.3
  12.5 0.3 reshape.89
  12.9 0.8 copy.10
  13.7 66.3 %gather_fusion = bf16[32640,32]{1,0:T(8,128)(2,1)} fusion(bf16[32,128]{0,1:T(8,128)(2,1)S(1)} %copy.10, s32[32768]{0:T(1024)S(1)} %pad_clamp_fusion), kind=kCustom, calls=%fused_computation | custom fusion | bytes 4308480 | tf_op jit(solution)/shard_map/jit(_take)/gather | solution.py:28
  80.0 6.9 %copy.11 = bf16[32640,32]{0,1:T(8,128)(2,1)S(1)} copy(bf16[32640,32]{1,0:T(8,128)(2,1)} %gather_fusion) | data formatting | bytes 4177920 | tf_op jit(solution)/shard_map/jit(_take)/gather | solution.py:28
  86.8 7.8 %reshape.92 = bf16[128,255,32]{1,0,2:T(8,128)(2,1)} reshape(bf16[32640,32]{0,1:T(8,128)(2,1)S(1)} %copy.11) | data formatting | bytes 4177920 | tf_op jit(solution)/shard_map/jit(_take)/gather | solution.py:28
  94.7 0.0 copy-start.1
  94.7 0.1 fusion.10
  94.8 1.9 select_bitcast_fusion
  96.7 0.0 collective-permute-done
  96.7 0.0 copy-done.1
  96.7 0.6 maximum_convert_fusion
  97.3 1.2 fusion
  98.5 0.0 copy-start
  98.5 1.9 copy-done
  100.3 0.2 fusion.5
  100.5 12.0 %while.10 = (s32[]{:T(128)}, f32[4,128,512]{2,1,0:T(8,128)}, s32[4]{0:T(128)S(1)}, bf16[639,512]{1,0:T(8,128)(2,1)S(1)}, bf16[32,128,255]{2,1,0:T(8,128)(2,1)S(1...) while((s32[]{:T(128)}, f32[4,128,512]{2,1,0:T(8,128)}, s32[4]{0:T(128)S(1)}, ...), condition=%wide.region_1.2_spmd, body=%wide.region_0.1_spmd.sunk | while | flops 33423364 | bytes 4705947 | solution.py:45
  100.5 0.6 dynamic_slice.11
  101.8 0.1 constant_dynamic-slice_fusion.2
  101.9 0.1 copy.20
  102.0 0.7 fusion.22
  102.7 0.1 copy.21
  102.8 0.7 constant_dynamic-update-slice_fusion.2
  103.5 0.6 dynamic_slice.11
  104.8 0.1 constant_dynamic-slice_fusion.2
  104.9 0.1 copy.20
  105.0 0.6 fusion.22
  105.7 0.2 copy.21
  105.8 0.8 constant_dynamic-update-slice_fusion.2
  106.6 0.6 dynamic_slice.11
  107.8 0.1 constant_dynamic-slice_fusion.2
  107.9 0.1 copy.20
  108.0 0.6 fusion.22
  108.7 0.2 copy.21
  108.8 0.7 constant_dynamic-update-slice_fusion.2
  109.6 0.6 dynamic_slice.11
  110.8 0.1 constant_dynamic-slice_fusion.2
  110.9 0.1 copy.20
  111.1 0.6 fusion.22
  111.7 0.2 copy.21
  111.8 0.7 constant_dynamic-update-slice_fusion.2
  112.6 1.8 fusion.4
  114.4 0.2 copy.14
  114.6 0.4 stack.2
  115.0 125.6 %all_to_all.5 = bf16[8,512,512]{1,2,0:T(8,128)(2,1)} all-to-all(bf16[8,512,512]{1,2,0:T(8,128)(2,1)S(1)} %stack.2), channel_id=1, replica_groups=mesh['seq'=64,'width'=8] {'width'}, dimensions={0} | all-to-all | bytes 8388608 | tf_op jit(solution)/shard_map/all_to_all | solution.py:61
  240.5 0.0 all-gather.2.cloned.1.call-done
  240.6 6.6 %convolution_convert_fusion = bf16[512,512]{1,0:T(8,128)(2,1)} fusion(bf16[512,4096]{0,1:T(8,128)(2,1)} %bitcast.46, bf16[4096,512]{1,0:T(8,128)(2,1)} %all-gather.2.cloned.1.call-done), kind=kOutput, calls=%fused_computation.12 | convolution fusion | flops 2147745792 | bytes 8912896 | tf_op jit(solution)/shard_map/dot_general | solution.py:63
  (4 shorter events, 0.1 us)
Async XLA Ops:
  6.5 234.0 %all-gather.2.cloned.1.call-start = ((), (), s32[]{:S(2)}) async-start(), calls=%async_computation.1 | async-start | bytes 4259840 | tf_op jit(solution)/shard_map/all_gather | solution.py:65
  7.6 89.1 %collective-permute-start = (bf16[129,3,512]{2,0,1:T(8,128)(2,1)S(1)}, bf16[129,3,512]{2,0,1:T(8,128)(2,1)S(1)}, u32[]{:S(2)}, u32[]{:S(2)}) collective-permute-start(bf16[129,3,512]{2,0,1:T(8,128)(2,1)S(1)} %slice.31), channel_id=1, source_target_pairs={{0,8},{8,16},{16,24},{24,32},{32,40},{40,48},{48,56},{56,64},{64,7... | collective-permute-start | bytes 1188872 | tf_op jit(solution)/shard_map/ppermute | solution.py:10
  94.7 2.1 copy-start.1
  98.5 1.9 copy-start
Sparse Core Ops, SparseCore 0:
  11.9 160.3 all-gather.1
